TPU v7x, 512 devices: a whole 4x4x16 slice. The times are simulated.
512 devices in a mesh: docs: 16 (over y, x), supp: 32 (over z, core).
Axes of the slice: x: 4, y: 4, z: 16, core: 2. Of those that a mesh axis runs over, the one named last changes fastest.
Arguments:
- vocab_table: bfloat16 [100000, 300], P('docs'), may hold values from -0.69140625 to 0.69140625
- support_atoms: bfloat16 [65536, 300], P('supp'), may hold values from -0.69140625 to 0.69140625
- weight_logits: float32 [65536], P('supp'), may hold values from -6 to 6
- word_counts: int32 [32], P('docs'), may hold values from 1 to 600, 11520 in all
- word_shard: int32 [20480, 1], P('docs'), may hold values from 0 to 15; in each aligned block of 1280 rows (0 to 1279, 1280 to 2559, ...) at most 128 rows name the same one
- word_row: int32 [20480], P('docs'), may hold values from 0 to 6249
Outputs:
- row_potential: float32 [32, 640], P('docs')
- col_potential: float32 [32, 65536], P('docs', 'supp')
- new_log_weights: float32 [65536], P('supp')
Inputs may be any that keep to these rules, and one draw needn't show every extreme that they name: `word_shard`: within the 1280 word slots of each index of docs (aligned blocks), no shard number appears more than 128 times, and some number appears exactly 128 times. `word_counts`: the longest document has exactly 600 words.
All inputs are finite; a program needn't handle non-finite values. No bound on the sum of `word_counts` on one device may be relied on, other than what follows from the above.
Results may differ from a plain program's by a relative error of at most 0.0003.
Values may be sent and summed in bfloat16 or wider, within the bound.
No kernel may reach another device: no remote copies, remote signals or barrier semaphores. Data moves between devices by JAX's collectives and lax.ppermute only.
A program may use at most 64 MiB of HBM per device.

v0:
```python
import jax
import jax.numpy as jnp
from jax import lax
from jax.sharding import PartitionSpec as P

ITERS = 2
epsilon = 0.05


def extent_supp(largest, summed):
    global_max = lax.pmax(largest, "supp")
    global_sum = lax.psum(summed * jnp.exp(largest - global_max), "supp")
    return global_max + jnp.log(global_sum)


def fetch_rows(requests, vocab_table):
    return lax.all_to_all(
        vocab_table[lax.all_to_all(requests, "docs", split_axis=0, concat_axis=0, tiled=True)],
        "docs",
        split_axis=0,
        concat_axis=0,
        tiled=True,
    )


def shards(vocab_table, support_atoms, weight_logits, word_counts, word_shard, word_row):
    groups = lax.axis_size("docs")
    supp_count = lax.axis_size("supp")
    docs_here = word_counts.shape[0]
    slot_count = word_row.shape[0]
    doc_slots = slot_count // docs_here
    atom_count = support_atoms.shape[0]
    capacity = supp_count * (
        (5 * slot_count + 4 * groups * supp_count - 1) // (4 * groups * supp_count)
    )
    word_owner = word_shard[:, 0]
    member = (word_owner[:, None] == jnp.arange(groups, dtype=jnp.int32)[None, :]).astype(jnp.int32)
    slot_rank = jnp.sum((jnp.cumsum(member, axis=0) - 1) * member, axis=1)
    requests = jnp.zeros((groups, capacity), jnp.int32).at[word_owner, slot_rank].set(word_row)
    fetched = fetch_rows(requests, vocab_table)
    word_vecs = fetched[word_owner, slot_rank]
    words_sq = jnp.sum(jnp.square(word_vecs.astype(jnp.float32)), axis=1).reshape(
        docs_here, doc_slots
    )
    atoms_sq = jnp.sum(jnp.square(support_atoms.astype(jnp.float32)), axis=1)
    product = jnp.dot(word_vecs, support_atoms.T, preferred_element_type=jnp.float32)
    product = product.reshape(docs_here, doc_slots, atom_count)
    stored = words_sq[:, :, None] + atoms_sq[None, None, :] - 2.0 * product
    logit_max = jnp.max(weight_logits)
    logit_sum = jnp.sum(jnp.exp(weight_logits - logit_max))
    log_base = weight_logits - extent_supp(logit_max, logit_sum)
    live_mask = jnp.arange(doc_slots)[None, :] < word_counts[:, None]
    log_share = -epsilon * jnp.log(word_counts.astype(jnp.float32))

    def column_extent(row_pot, dist_grid):
        scores = (row_pot[:, :, None] - dist_grid) / epsilon
        largest = jnp.max(jnp.where(live_mask[:, :, None], scores, -jnp.inf), axis=1)
        summed = jnp.sum(
            jnp.where(live_mask[:, :, None], jnp.exp(scores - largest[:, None, :]), 0.0), axis=1
        )
        return largest + jnp.log(summed)

    row_pot = jnp.zeros((docs_here, doc_slots), jnp.float32)
    col_pot = jnp.zeros((docs_here, atom_count), jnp.float32)
    for sweep in range(ITERS):
        dist_grid = stored
        col_pot = epsilon * log_base[None, :] - epsilon * column_extent(row_pot, dist_grid)
        scores = (col_pot[:, None, :] - dist_grid) / epsilon
        largest = jnp.max(scores, axis=2)
        summed = jnp.sum(jnp.exp(scores - largest[:, :, None]), axis=2)
        row_ext = extent_supp(largest, summed)
        row_pot = jnp.where(live_mask, log_share[:, None] - epsilon * row_ext, 0.0)
    dist_grid = stored
    log_marg = col_pot / epsilon + column_extent(row_pot, dist_grid)
    grand_total = lax.psum(jnp.sum(log_marg, axis=0), "docs")
    mean_log = grand_total / (docs_here * groups)
    mean_max = jnp.max(mean_log)
    mean_sum = jnp.sum(jnp.exp(mean_log - mean_max))
    new_log = mean_log - extent_supp(mean_max, mean_sum)
    return (row_pot, col_pot, new_log)


def solution(mesh):
    placed = (P("docs", None), P("supp", None), P("supp"), P("docs"), P("docs", None), P("docs"))
    return jax.shard_map(
        shards,
        mesh=mesh,
        in_specs=placed,
        out_specs=(P("docs", None), P("docs", "supp"), P("supp")),
        check_vma=False,
    )
```

profile of v0, /device:TPU:1, one launch (start us, length us, event | category | flops | bytes accessed | tf_op | source)
XLA Modules:
  0.0 547.9 jit_solution(805814266147628978)
XLA Ops:
  0.6 0.7 reduce.6
  1.4 4.5 reduce-window.6
  5.9 0.4 slice_reduce_fusion
  6.3 0.2 reduce-window.9
  6.5 0.1 add_add_fusion
  6.7 0.7 or_reduce_fusion
  7.4 0.7 multiply_reduce_fusion.2
  8.1 0.8 and_reduce_fusion
  8.9 6.0 %scatter_custom_fusion = s32[2048]{0:T(1024)} fusion(s32[1280]{0:T(1024)S(1)} %broadcast_select_fusion, s32[1280]{0:T(1024)} %param.11, s32[]{:T(128)} %constant.16.clone.1), kind=kCustom, calls=%fused_computation.55 | custom fusion | bytes 8704
  14.9 7.6 %all-to-all-start = ((s32[16,1,128]{2,1,0:T(1,128)}), s32[16,1,128]{2,1,0:T(1,128)S(1)}, u32[]{:S(2)}, u32[]{:S(2)}) async-start(s32[16,1,128]{2,1,0:T(1,128)} %bitcast.1), calls=%async_computation | async-start | bytes 16384 | tf_op jit(solution)/shard_map/all_to_all | solution.py:18
  22.5 7.1 %copy.11 = bf16[6250,300]{1,0:T(8,128)(2,1)} copy(bf16[6250,300]{0,1:T(8,128)(2,1)} %param.6) | data formatting | bytes 7500000 | tf_op args[0]
  29.6 10.3 %gather_fusion = bf16[2048,300]{1,0:T(8,128)(2,1)S(1)} fusion(bf16[6250,300]{1,0:T(8,128)(2,1)} %copy.11, s32[2048]{0:T(1024)S(1)} %fusion.8), kind=kCustom, calls=%fused_computation | custom fusion | bytes 2465792 | tf_op jit(solution)/shard_map/gather | solution.py:18
  39.9 1.6 copy.12
  41.5 6.7 %all-to-all-start.1 = ((bf16[16,128,300]{1,2,0:T(8,128)(2,1)}), bf16[16,128,300]{1,2,0:T(8,128)(2,1)}, u32[]{:S(2)}, u32[]{:S(2)}) async-start(bf16[16,128,300]{1,2,0:T(8,128)(2,1)} %copy.12), calls=%async_computation.1 | async-start | bytes 2490368 | tf_op jit(solution)/shard_map/all_to_all | solution.py:17
  48.2 0.6 reduce_max.67
  48.8 54.7 %pmax.28 = f32[]{:T(128)} all-reduce(f32[]{:T(128)} %reduce_max.67), channel_id=1, replica_groups=mesh['docs'=16,'supp'=32] {'supp'}, use_global_device_ids=true, to_apply=%region_1.2 | all-reduce | flops 1 | bytes 8 | tf_op jit(solution)/shard_map/pmax | solution.py:11
  104.9 1.3 exponential_reduce_fusion.3
  106.8 47.9 %psum.35 = f32[]{:T(128)} all-reduce(f32[]{:T(128)S(6)} %mul.57), channel_id=1, replica_groups=mesh['docs'=16,'supp'=32] {'supp'}, use_global_device_ids=true, to_apply=%region_3.4 | all-reduce | flops 1 | bytes 8 | tf_op jit(solution)/shard_map/psum | solution.py:12
  156.1 0.3 multiply_reduce_fusion
  156.4 0.1 iota_compare_fusion.2
  156.4 1.8 copy.13
  158.3 8.1 %gather_fusion.1 = bf16[1280,300]{1,0:T(8,128)(2,1)S(1)} fusion(bf16[16,128,300]{2,1,0:T(8,128)(2,1)S(1)} %copy.13, s32[1280]{0:T(1024)S(1)} %get-tuple-element.3), kind=kCustom, calls=%fused_computation.1 | custom fusion | bytes 1546240 | tf_op jit(solution)/shard_map/gather | solution.py:41
  166.4 6.8 %convolution_multiply_fusion = f32[1280,2048]{1,0:T(8,128)} fusion(bf16[1280,300]{1,0:T(8,128)(2,1)S(1)} %gather_fusion.1, bf16[2048,300]{0,1:T(8,128)(2,1)} %param.7), kind=kOutput, calls=%fused_computation.20 | convolution fusion | flops 1575485440 | bytes 12482560 | tf_op jit(solution)/shard_map/dot_general | solution.py:46
  173.2 0.3 multiply_reduce_fusion.1
  173.5 6.1 %select_reduce_fusion.5 = f32[2,2048]{1,0:T(2,128)S(1)} fusion(pred[2,640]{1,0:T(4,128)(4,1)S(1)} %iota_compare_fusion.2, f32[2,640,2048]{2,1,0:T(8,128)} %bitcast.41, f32[2048]{0:T(1024)S(1)} %multiply_reduce_fusion, f32[2,640]{1,0:T(2,128)S(1)} %add.104), kind=kLoop, calls=%fused_computation.17 | loop fusion | flops 15724544 | bytes 10516736 | tf_op jit(solution)/shard_map/reduce_max | solution.py:57
  179.6 0.9 copy-done
  180.5 4.1 select_reduce_fusion.4
  184.7 2.1 fusion.2
  186.7 3.0 exponential_reduce_fusion.1
  189.7 46.8 %pmax.29 = f32[2,640]{1,0:T(2,128)S(1)} all-reduce(f32[2,640]{1,0:T(2,128)S(1)} %reduce_max.70), channel_id=1, replica_groups=mesh['docs'=16,'supp'=32] {'supp'}, use_global_device_ids=true, to_apply=%region_13.14 | all-reduce | flops 1280 | bytes 10240 | tf_op jit(solution)/shard_map/pmax | solution.py:11
  236.5 47.0 %psum.36 = f32[2,640]{1,0:T(2,128)S(1)} all-reduce(f32[2,640]{1,0:T(2,128)S(1)} %exponential_multiply_fusion.1), channel_id=1, replica_groups=mesh['docs'=16,'supp'=32] {'supp'}, use_global_device_ids=true, to_apply=%region_15.16 | all-reduce | flops 1280 | bytes 10240 | tf_op jit(solution)/shard_map/psum | solution.py:12
  283.6 0.1 subtract_select_fusion.1
  283.6 6.7 %select_reduce_fusion.3 = f32[2,2048]{1,0:T(2,128)S(1)} fusion(f32[2,640]{1,0:T(2,128)S(1)} %subtract_select_fusion.1, pred[2,640]{1,0:T(4,128)(4,1)S(1)} %iota_compare_fusion.2, f32[2,640,2048]{2,1,0:T(8,128)} %bitcast.42, f32[2048]{0:T(1024)S(1)} %multiply_reduce_fusion, f32[2,640]{1,0:T(2,128)S(1)} %add.104), kind=kLoop, calls=%fused_computation.12 | loop fusion | flops 15724544 | bytes 10521856 | tf_op jit(solution)/shard_map/reduce_max | solution.py:57
  290.4 6.8 %select_reduce_fusion.2 = f32[2,2048]{1,0:T(2,128)S(1)} fusion(f32[2,2048]{1,0:T(2,128)S(1)} %select_reduce_fusion.3, f32[2,640]{1,0:T(2,128)S(1)} %subtract_select_fusion.1, pred[2,640]{1,0:T(4,128)(4,1)S(1)} %iota_compare_fusion.2, f32[2,640,2048]{2,1,0:T(8,128)} %bitcast.43, f32[2048]{0:T(1024)S(1)} %multiply_reduce_fusion, f32[2,640]{1,0:T(2,128)S(1)} %add.104), kind=kLoop, calls=%fused_computation.11 | loop fusion | flops 18345984 | bytes 10538240 | tf_op jit(solution)/shard_map/reduce_sum | solution.py:58
  297.2 0.0 copy-start.2
  297.2 2.1 fusion.3
  299.3 3.0 exponential_reduce_fusion
  302.3 46.8 %pmax.30 = f32[2,640]{1,0:T(2,128)S(1)} all-reduce(f32[2,640]{1,0:T(2,128)S(1)} %reduce_max.73), channel_id=1, replica_groups=mesh['docs'=16,'supp'=32] {'supp'}, use_global_device_ids=true, to_apply=%region_19.20 | all-reduce | flops 1280 | bytes 10240 | tf_op jit(solution)/shard_map/pmax | solution.py:11
  349.1 46.8 %psum.37 = f32[2,640]{1,0:T(2,128)S(1)} all-reduce(f32[2,640]{1,0:T(2,128)S(1)} %exponential_multiply_fusion), channel_id=1, replica_groups=mesh['docs'=16,'supp'=32] {'supp'}, use_global_device_ids=true, to_apply=%region_21.22 | all-reduce | flops 1280 | bytes 10240 | tf_op jit(solution)/shard_map/psum | solution.py:12
  395.9 0.1 subtract_select_fusion
  396.0 5.8 %select_reduce_fusion.1 = f32[2,2048]{1,0:T(2,128)S(1)} fusion(f32[2,640]{1,0:T(2,128)S(1)} %subtract_select_fusion, pred[2,640]{1,0:T(4,128)(4,1)S(1)} %iota_compare_fusion.2, f32[2,640,2048]{2,1,0:T(8,128)} %bitcast.44, f32[2048]{0:T(1024)S(1)} %multiply_reduce_fusion, f32[2,640]{1,0:T(2,128)S(1)} %add.104), kind=kLoop, calls=%fused_computation.8 | loop fusion | flops 15724544 | bytes 10521856 | tf_op jit(solution)/shard_map/reduce_max | solution.py:57
  401.7 6.6 %select_reduce_fusion = f32[2,2048]{1,0:T(2,128)S(1)} fusion(f32[2,2048]{1,0:T(2,128)S(1)} %select_reduce_fusion.1, f32[2,640]{1,0:T(2,128)S(1)} %subtract_select_fusion, pred[2,640]{1,0:T(4,128)(4,1)S(1)} %iota_compare_fusion.2, f32[2,640,2048]{2,1,0:T(8,128)} %bitcast.45, f32[2048]{0:T(1024)S(1)} %multiply_reduce_fusion, f32[2,640]{1,0:T(2,128)S(1)} %add.104), kind=kLoop, calls=%fused_computation.7 | loop fusion | flops 18345984 | bytes 10538240 | tf_op jit(solution)/shard_map/reduce_sum | solution.py:58
  408.4 33.7 %psum.38 = f32[2048]{0:T(1024)S(1)} all-reduce(f32[2048]{0:T(1024)S(1)} %add_reduce_fusion), channel_id=1, replica_groups=mesh['docs'=16,'supp'=32] {'docs'}, use_global_device_ids=true, to_apply=%region_25.26 | all-reduce | flops 2048 | bytes 16384 | tf_op jit(solution)/shard_map/psum | solution.py:75
  442.1 0.6 multiply_reduce_fusion.3
  442.7 53.8 %pmax.31 = f32[]{:T(128)} all-reduce(f32[]{:T(128)} %multiply_reduce_fusion.3), channel_id=1, replica_groups=mesh['docs'=16,'supp'=32] {'supp'}, use_global_device_ids=true, to_apply=%region_27.28 | all-reduce | flops 1 | bytes 8 | tf_op jit(solution)/shard_map/pmax | solution.py:11
  496.4 1.2 exponential_reduce_fusion.2
  499.6 46.3 %psum.39 = f32[]{:T(128)} all-reduce(f32[]{:T(128)S(6)} %mul.69), channel_id=1, replica_groups=mesh['docs'=16,'supp'=32] {'supp'}, use_global_device_ids=true, to_apply=%region_29.30 | all-reduce | flops 1 | bytes 8 | tf_op jit(solution)/shard_map/psum | solution.py:12
  547.3 0.6 multiply_subtract_fusion.2
  (35 shorter events, 0.3 us)
Async XLA Ops:
  14.9 14.7 %all-to-all-start = ((s32[16,1,128]{2,1,0:T(1,128)}), s32[16,1,128]{2,1,0:T(1,128)S(1)}, u32[]{:S(2)}, u32[]{:S(2)}) async-start(s32[16,1,128]{2,1,0:T(1,128)} %bitcast.1), calls=%async_computation | async-start | bytes 16384 | tf_op jit(solution)/shard_map/all_to_all | solution.py:18
  29.6 18.6 %copy-start.3 = (f32[2048]{0:T(1024)S(1)}, f32[2048]{0:T(1024)}, u32[]{:S(2)}) copy-start(f32[2048]{0:T(1024)} %param.8) | copy-start | bytes 24580
  29.6 126.4 %copy-start.1 = (bf16[2048,300]{0,1:T(8,128)(2,1)S(1)}, bf16[2048,300]{0,1:T(8,128)(2,1)}, u32[]{:S(2)}) copy-start(bf16[2048,300]{0,1:T(8,128)(2,1)} %param.7) | copy-start | bytes 3686404
  29.6 126.7 %copy-start.5 = (s32[2]{0:T(128)S(1)}, s32[2]{0:T(128)}, u32[]{:S(2)}) copy-start(s32[2]{0:T(128)} %param.9) | copy-start | bytes 28
  41.5 114.9 %all-to-all-start.1 = ((bf16[16,128,300]{1,2,0:T(8,128)(2,1)}), bf16[16,128,300]{1,2,0:T(8,128)(2,1)}, u32[]{:S(2)}, u32[]{:S(2)}) async-start(bf16[16,128,300]{1,2,0:T(8,128)(2,1)} %copy.12), calls=%async_computation.1 | async-start | bytes 2490368 | tf_op jit(solution)/shard_map/all_to_all | solution.py:17
  173.5 7.0 %copy-start = (f32[1280,2048]{1,0:T(8,128)S(1)}, f32[1280,2048]{1,0:T(8,128)}, u32[]{:S(2)}) copy-start(f32[1280,2048]{1,0:T(8,128)} %convolution_multiply_fusion) | copy-start | bytes 31457284
  283.6 13.5 %slice-start = ((s8[10485760]{0:T(1024)(128)(4,1)}), s8[4194304]{0:T(1024)(128)(4,1)S(1)}, s32[]{:S(2)}) async-start(s8[10485760]{0:T(1024)(128)(4,1)} %bitcast.47), calls=%async_computation.2 | async-start | bytes 8388608
  283.6 13.5 %slice-start.1 = ((s8[10485760]{0:T(1024)(128)(4,1)}), s8[4194304]{0:T(1024)(128)(4,1)S(1)}, s32[]{:S(2)}) async-start(s8[10485760]{0:T(1024)(128)(4,1)} %bitcast.47), calls=%async_computation.3 | async-start | bytes 8388608
  290.3 6.8 %slice-start.2 = ((s8[10485760]{0:T(1024)(128)(4,1)}), s8[2097152]{0:T(1024)(128)(4,1)S(1)}, s32[]{:S(2)}) async-start(s8[10485760]{0:T(1024)(128)(4,1)} %bitcast.47), calls=%async_computation.4 | async-start | bytes 4194304
  297.2 111.2 %copy-start.2 = (f32[2,2048]{1,0:T(2,128)}, f32[2,2048]{1,0:T(2,128)S(1)}, u32[]{:S(2)}) copy-start(f32[2,2048]{1,0:T(2,128)S(1)} %multiply_subtract_fusion) | copy-start | bytes 49156
  396.0 12.4 %copy-start.4 = (f32[2,640]{1,0:T(2,128)}, f32[2,640]{1,0:T(2,128)S(1)}, u32[]{:S(2)}) copy-start(f32[2,640]{1,0:T(2,128)S(1)} %subtract_select_fusion) | copy-start | bytes 15364
where the time goes:
time: 549 us; the launch traced here: 548 us
  blocking collectives  424 us (77%)
  other arithmetic  59.1 us (11%)
  local copies, waits for them, and re-layouts  36.3 us (7%)
  starting transfers between devices  14.3 us (3%)
  between operations  7.63 us (1%)
  matrix products  6.83 us (1%)
    pmax x4, blocking collectives, extent_supp(): global_max = lax.pmax(largest, 'supp')  202 us
    psum x4, blocking collectives, extent_supp(): global_sum = lax.psum(summed * jnp.exp(largest - global_max), 'supp')  188 us
    psum x1, blocking collectives, shards(): grand_total = lax.psum(jnp.sum(log_marg, axis=0), 'docs')  33.7 us
    reduce_max x3, other arithmetic, column_extent(): jnp.max(jnp.where(live_mask[:, :, None], scores, -jnp.inf), axis=1)  18.5 us
    reduce_sum x3, other arithmetic, column_extent(): jnp.sum(jnp.where(live_mask[:, :, None], jnp.exp(scores - largest[:, None...  17.5 us
    unnamed x20, local copies, waits for them, and re-layouts  14.1 us
    gather x2, local copies, waits for them, and re-layouts, fetch_rows(): vocab_table[lax.all_to_all(requests, 'docs', split_axis=0, concat_axis=0,...  11.9 us
  transfers between devices with their start and end apart: 2, of which 0 were waited for; matrix products, arithmetic and copies ran while one was open for 2% of the time, Pallas kernels for 0%

commit v1 on v0

--- a/solution.py
+++ b/solution.py
@@ -72,7 +72,9 @@
         row_pot = jnp.where(live_mask, log_share[:, None] - epsilon * row_ext, 0.0)
     dist_grid = stored
     log_marg = col_pot / epsilon + column_extent(row_pot, dist_grid)
-    grand_total = lax.psum(jnp.sum(log_marg, axis=0), "docs")
+    own = jnp.sum(log_marg, axis=0)
+    parts = lax.all_gather(own, "docs", axis=0, tiled=False)
+    grand_total = parts.sum(axis=0)
     mean_log = grand_total / (docs_here * groups)
     mean_max = jnp.max(mean_log)
     mean_sum = jnp.sum(jnp.exp(mean_log - mean_max))

time: 549 us -> 532 us (0.969)
  blocking collectives: 424 us -> 407 us
    psum x1 -> x0, blocking collectives: 33.7 us -> none  [shards(): grand_total = lax.psum(jnp.sum(log_marg, axis=0), 'docs')]
    all_gather x0 -> x1, blocking collectives: none -> 18.6 us  [shards(): parts = lax.all_gather(own, 'docs', axis=0, tiled=False)]
where the time goes in v1:
time: 532 us; the launch traced here: 531 us
  blocking collectives  407 us (77%)
  other arithmetic  59.1 us (11%)
  local copies, waits for them, and re-layouts  36.4 us (7%)
  starting transfers between devices  14.3 us (3%)
  between operations  7.63 us (1%)
  matrix products  6.83 us (1%)
    pmax x4, blocking collectives, extent_supp(): global_max = lax.pmax(largest, 'supp')  200 us
    psum x4, blocking collectives, extent_supp(): global_sum = lax.psum(summed * jnp.exp(largest - global_max), 'supp')  188 us
    all_gather x1, blocking collectives, shards(): parts = lax.all_gather(own, 'docs', axis=0, tiled=False)  18.6 us
    reduce_max x3, other arithmetic, column_extent(): jnp.max(jnp.where(live_mask[:, :, None], scores, -jnp.inf), axis=1)  18.5 us
    reduce_sum x3, other arithmetic, column_extent(): jnp.sum(jnp.where(live_mask[:, :, None], jnp.exp(scores - largest[:, None...  17.5 us
    unnamed x20, local copies, waits for them, and re-layouts  14.1 us
    gather x2, local copies, waits for them, and re-layouts, fetch_rows(): vocab_table[lax.all_to_all(requests, 'docs', split_axis=0, concat_axis=0,...  11.9 us
  transfers between devices with their start and end apart: 2, of which 0 were waited for; matrix products, arithmetic and copies ran while one was open for 2% of the time, Pallas kernels for 0%

profile of v1, /device:TPU:1, one launch (start us, length us, event | category | flops | bytes accessed | tf_op | source)
XLA Modules:
  0.0 530.8 jit_solution(18399695450374558582)
XLA Ops:
  0.6 0.7 reduce.6
  1.4 4.5 reduce-window.6
  5.9 0.4 slice_reduce_fusion
  6.3 0.2 reduce-window.9
  6.5 0.1 add_add_fusion
  6.7 0.7 or_reduce_fusion
  7.4 0.7 multiply_reduce_fusion.2
  8.1 0.8 and_reduce_fusion
  8.9 6.0 %scatter_custom_fusion = s32[2048]{0:T(1024)} fusion(s32[1280]{0:T(1024)S(1)} %broadcast_select_fusion, s32[1280]{0:T(1024)} %param.11, s32[]{:T(128)} %constant.16.clone.1), kind=kCustom, calls=%fused_computation.55 | custom fusion | bytes 8704
  14.9 7.6 %all-to-all-start = ((s32[16,1,128]{2,1,0:T(1,128)}), s32[16,1,128]{2,1,0:T(1,128)S(1)}, u32[]{:S(2)}, u32[]{:S(2)}) async-start(s32[16,1,128]{2,1,0:T(1,128)} %bitcast.1), calls=%async_computation | async-start | bytes 16384 | tf_op jit(solution)/shard_map/all_to_all | solution.py:18
  22.5 7.1 %copy.14 = bf16[6250,300]{1,0:T(8,128)(2,1)} copy(bf16[6250,300]{0,1:T(8,128)(2,1)} %param.6) | data formatting | bytes 7500000 | tf_op args[0]
  29.6 10.3 %gather_fusion = bf16[2048,300]{1,0:T(8,128)(2,1)S(1)} fusion(bf16[6250,300]{1,0:T(8,128)(2,1)} %copy.14, s32[2048]{0:T(1024)S(1)} %fusion.8), kind=kCustom, calls=%fused_computation | custom fusion | bytes 2465792 | tf_op jit(solution)/shard_map/gather | solution.py:18
  39.9 1.6 copy.15
  41.5 6.7 %all-to-all-start.1 = ((bf16[16,128,300]{1,2,0:T(8,128)(2,1)}), bf16[16,128,300]{1,2,0:T(8,128)(2,1)}, u32[]{:S(2)}, u32[]{:S(2)}) async-start(bf16[16,128,300]{1,2,0:T(8,128)(2,1)} %copy.15), calls=%async_computation.1 | async-start | bytes 2490368 | tf_op jit(solution)/shard_map/all_to_all | solution.py:17
  48.2 0.6 reduce_max.67
  48.8 54.7 %pmax.28 = f32[]{:T(128)} all-reduce(f32[]{:T(128)} %reduce_max.67), channel_id=1, replica_groups=mesh['docs'=16,'supp'=32] {'supp'}, use_global_device_ids=true, to_apply=%region_1.2 | all-reduce | flops 1 | bytes 8 | tf_op jit(solution)/shard_map/pmax | solution.py:11
  104.9 1.3 exponential_reduce_fusion.3
  106.8 47.9 %psum.28 = f32[]{:T(128)} all-reduce(f32[]{:T(128)S(6)} %mul.57), channel_id=1, replica_groups=mesh['docs'=16,'supp'=32] {'supp'}, use_global_device_ids=true, to_apply=%region_3.4 | all-reduce | flops 1 | bytes 8 | tf_op jit(solution)/shard_map/psum | solution.py:12
  156.1 0.3 multiply_reduce_fusion
  156.4 0.1 iota_compare_fusion.2
  156.4 1.8 copy.16
  158.3 8.1 %gather_fusion.1 = bf16[1280,300]{1,0:T(8,128)(2,1)S(1)} fusion(bf16[16,128,300]{2,1,0:T(8,128)(2,1)S(1)} %copy.16, s32[1280]{0:T(1024)S(1)} %get-tuple-element.3), kind=kCustom, calls=%fused_computation.1 | custom fusion | bytes 1546240 | tf_op jit(solution)/shard_map/gather | solution.py:41
  166.4 6.8 %convolution_multiply_fusion = f32[1280,2048]{1,0:T(8,128)} fusion(bf16[1280,300]{1,0:T(8,128)(2,1)S(1)} %gather_fusion.1, bf16[2048,300]{0,1:T(8,128)(2,1)} %param.7), kind=kOutput, calls=%fused_computation.20 | convolution fusion | flops 1575485440 | bytes 12482560 | tf_op jit(solution)/shard_map/dot_general | solution.py:46
  173.2 0.3 multiply_reduce_fusion.1
  173.5 6.1 %select_reduce_fusion.5 = f32[2,2048]{1,0:T(2,128)S(1)} fusion(pred[2,640]{1,0:T(4,128)(4,1)S(1)} %iota_compare_fusion.2, f32[2,640,2048]{2,1,0:T(8,128)} %bitcast.41, f32[2048]{0:T(1024)S(1)} %multiply_reduce_fusion, f32[2,640]{1,0:T(2,128)S(1)} %add.102), kind=kLoop, calls=%fused_computation.17 | loop fusion | flops 15724544 | bytes 10516736 | tf_op jit(solution)/shard_map/reduce_max | solution.py:57
  179.6 0.9 copy-done
  180.5 4.1 select_reduce_fusion.4
  184.7 2.1 fusion.2
  186.7 3.0 exponential_reduce_fusion.1
  189.7 46.8 %pmax.29 = f32[2,640]{1,0:T(2,128)S(1)} all-reduce(f32[2,640]{1,0:T(2,128)S(1)} %reduce_max.70), channel_id=1, replica_groups=mesh['docs'=16,'supp'=32] {'supp'}, use_global_device_ids=true, to_apply=%region_13.14 | all-reduce | flops 1280 | bytes 10240 | tf_op jit(solution)/shard_map/pmax | solution.py:11
  236.5 47.0 %psum.29 = f32[2,640]{1,0:T(2,128)S(1)} all-reduce(f32[2,640]{1,0:T(2,128)S(1)} %exponential_multiply_fusion.1), channel_id=1, replica_groups=mesh['docs'=16,'supp'=32] {'supp'}, use_global_device_ids=true, to_apply=%region_15.16 | all-reduce | flops 1280 | bytes 10240 | tf_op jit(solution)/shard_map/psum | solution.py:12
  283.5 0.1 subtract_select_fusion.1
  283.6 6.7 %select_reduce_fusion.3 = f32[2,2048]{1,0:T(2,128)S(1)} fusion(f32[2,640]{1,0:T(2,128)S(1)} %subtract_select_fusion.1, pred[2,640]{1,0:T(4,128)(4,1)S(1)} %iota_compare_fusion.2, f32[2,640,2048]{2,1,0:T(8,128)} %bitcast.42, f32[2048]{0:T(1024)S(1)} %multiply_reduce_fusion, f32[2,640]{1,0:T(2,128)S(1)} %add.102), kind=kLoop, calls=%fused_computation.12 | loop fusion | flops 15724544 | bytes 10521856 | tf_op jit(solution)/shard_map/reduce_max | solution.py:57
  290.3 6.7 %select_reduce_fusion.2 = f32[2,2048]{1,0:T(2,128)S(1)} fusion(f32[2,2048]{1,0:T(2,128)S(1)} %select_reduce_fusion.3, f32[2,640]{1,0:T(2,128)S(1)} %subtract_select_fusion.1, pred[2,640]{1,0:T(4,128)(4,1)S(1)} %iota_compare_fusion.2, f32[2,640,2048]{2,1,0:T(8,128)} %bitcast.43, f32[2048]{0:T(1024)S(1)} %multiply_reduce_fusion, f32[2,640]{1,0:T(2,128)S(1)} %add.102), kind=kLoop, calls=%fused_computation.11 | loop fusion | flops 18345984 | bytes 10538240 | tf_op jit(solution)/shard_map/reduce_sum | solution.py:58
  297.2 0.0 copy-start.2
  297.2 2.1 fusion.3
  299.2 3.0 exponential_reduce_fusion
  302.2 46.8 %pmax.30 = f32[2,640]{1,0:T(2,128)S(1)} all-reduce(f32[2,640]{1,0:T(2,128)S(1)} %reduce_max.73), channel_id=1, replica_groups=mesh['docs'=16,'supp'=32] {'supp'}, use_global_device_ids=true, to_apply=%region_19.20 | all-reduce | flops 1280 | bytes 10240 | tf_op jit(solution)/shard_map/pmax | solution.py:11
  349.1 46.8 %psum.30 = f32[2,640]{1,0:T(2,128)S(1)} all-reduce(f32[2,640]{1,0:T(2,128)S(1)} %exponential_multiply_fusion), channel_id=1, replica_groups=mesh['docs'=16,'supp'=32] {'supp'}, use_global_device_ids=true, to_apply=%region_21.22 | all-reduce | flops 1280 | bytes 10240 | tf_op jit(solution)/shard_map/psum | solution.py:12
  395.9 0.1 subtract_select_fusion
  395.9 5.8 %select_reduce_fusion.1 = f32[2,2048]{1,0:T(2,128)S(1)} fusion(f32[2,640]{1,0:T(2,128)S(1)} %subtract_select_fusion, pred[2,640]{1,0:T(4,128)(4,1)S(1)} %iota_compare_fusion.2, f32[2,640,2048]{2,1,0:T(8,128)} %bitcast.44, f32[2048]{0:T(1024)S(1)} %multiply_reduce_fusion, f32[2,640]{1,0:T(2,128)S(1)} %add.102), kind=kLoop, calls=%fused_computation.8 | loop fusion | flops 15724544 | bytes 10521856 | tf_op jit(solution)/shard_map/reduce_max | solution.py:57
  401.7 6.6 %select_reduce_fusion = f32[2,2048]{1,0:T(2,128)S(1)} fusion(f32[2,2048]{1,0:T(2,128)S(1)} %select_reduce_fusion.1, f32[2,640]{1,0:T(2,128)S(1)} %subtract_select_fusion, pred[2,640]{1,0:T(4,128)(4,1)S(1)} %iota_compare_fusion.2, f32[2,640,2048]{2,1,0:T(8,128)} %bitcast.45, f32[2048]{0:T(1024)S(1)} %multiply_reduce_fusion, f32[2,640]{1,0:T(2,128)S(1)} %add.102), kind=kLoop, calls=%fused_computation.7 | loop fusion | flops 18345984 | bytes 10538240 | tf_op jit(solution)/shard_map/reduce_sum | solution.py:58
  408.4 18.6 %all-gather = f32[32768]{0:T(1024)S(1)} all-gather(f32[2048]{0:T(1024)S(1)} %add_reduce_fusion), channel_id=2, replica_groups=mesh['docs'=16,'supp'=32] {'docs'}, dimensions={0}, use_global_device_ids=true | all-gather | bytes 139264 | tf_op jit(solution)/shard_map/all_gather | solution.py:76
  427.0 0.6 multiply_reduce_fusion.3
  427.6 51.7 %pmax.31 = f32[]{:T(128)} all-reduce(f32[]{:T(128)} %multiply_reduce_fusion.3), channel_id=1, replica_groups=mesh['docs'=16,'supp'=32] {'supp'}, use_global_device_ids=true, to_apply=%region_27.28 | all-reduce | flops 1 | bytes 8 | tf_op jit(solution)/shard_map/pmax | solution.py:11
  479.4 1.2 exponential_reduce_fusion.2
  482.5 46.3 %psum.31 = f32[]{:T(128)} all-reduce(f32[]{:T(128)S(6)} %mul.69), channel_id=1, replica_groups=mesh['docs'=16,'supp'=32] {'supp'}, use_global_device_ids=true, to_apply=%region_29.30 | all-reduce | flops 1 | bytes 8 | tf_op jit(solution)/shard_map/psum | solution.py:12
  530.2 0.6 multiply_subtract_fusion.2
  (37 shorter events, 0.3 us)
Async XLA Ops:
  14.9 14.7 %all-to-all-start = ((s32[16,1,128]{2,1,0:T(1,128)}), s32[16,1,128]{2,1,0:T(1,128)S(1)}, u32[]{:S(2)}, u32[]{:S(2)}) async-start(s32[16,1,128]{2,1,0:T(1,128)} %bitcast.1), calls=%async_computation | async-start | bytes 16384 | tf_op jit(solution)/shard_map/all_to_all | solution.py:18
  29.6 18.6 %copy-start.3 = (f32[2048]{0:T(1024)S(1)}, f32[2048]{0:T(1024)}, u32[]{:S(2)}) copy-start(f32[2048]{0:T(1024)} %param.8) | copy-start | bytes 24580
  29.6 126.4 %copy-start.1 = (bf16[2048,300]{0,1:T(8,128)(2,1)S(1)}, bf16[2048,300]{0,1:T(8,128)(2,1)}, u32[]{:S(2)}) copy-start(bf16[2048,300]{0,1:T(8,128)(2,1)} %param.7) | copy-start | bytes 3686404
  29.6 126.7 %copy-start.5 = (s32[2]{0:T(128)S(1)}, s32[2]{0:T(128)}, u32[]{:S(2)}) copy-start(s32[2]{0:T(128)} %param.9) | copy-start | bytes 28
  41.5 114.9 %all-to-all-start.1 = ((bf16[16,128,300]{1,2,0:T(8,128)(2,1)}), bf16[16,128,300]{1,2,0:T(8,128)(2,1)}, u32[]{:S(2)}, u32[]{:S(2)}) async-start(bf16[16,128,300]{1,2,0:T(8,128)(2,1)} %copy.15), calls=%async_computation.1 | async-start | bytes 2490368 | tf_op jit(solution)/shard_map/all_to_all | solution.py:17
  173.5 7.0 %copy-start = (f32[1280,2048]{1,0:T(8,128)S(1)}, f32[1280,2048]{1,0:T(8,128)}, u32[]{:S(2)}) copy-start(f32[1280,2048]{1,0:T(8,128)} %convolution_multiply_fusion) | copy-start | bytes 31457284
  283.6 13.5 %slice-start = ((s8[10485760]{0:T(1024)(128)(4,1)}), s8[4194304]{0:T(1024)(128)(4,1)S(1)}, s32[]{:S(2)}) async-start(s8[10485760]{0:T(1024)(128)(4,1)} %bitcast.47), calls=%async_computation.2 | async-start | bytes 8388608
  283.6 13.5 %slice-start.1 = ((s8[10485760]{0:T(1024)(128)(4,1)}), s8[4194304]{0:T(1024)(128)(4,1)S(1)}, s32[]{:S(2)}) async-start(s8[10485760]{0:T(1024)(128)(4,1)} %bitcast.47), calls=%async_computation.3 | async-start | bytes 8388608
  290.3 6.8 %slice-start.2 = ((s8[10485760]{0:T(1024)(128)(4,1)}), s8[2097152]{0:T(1024)(128)(4,1)S(1)}, s32[]{:S(2)}) async-start(s8[10485760]{0:T(1024)(128)(4,1)} %bitcast.47), calls=%async_computation.4 | async-start | bytes 4194304
  297.2 111.2 %copy-start.2 = (f32[2,2048]{1,0:T(2,128)}, f32[2,2048]{1,0:T(2,128)S(1)}, u32[]{:S(2)}) copy-start(f32[2,2048]{1,0:T(2,128)S(1)} %multiply_subtract_fusion) | copy-start | bytes 49156
  395.9 12.4 %copy-start.4 = (f32[2,640]{1,0:T(2,128)}, f32[2,640]{1,0:T(2,128)S(1)}, u32[]{:S(2)}) copy-start(f32[2,640]{1,0:T(2,128)S(1)} %subtract_select_fusion) | copy-start | bytes 15364
